TPU v7x, 32 devices: a whole 2x2x4 slice. The times are simulated.
32 devices in a mesh: epoch: 4 (over z), vel: 8 (over y, x, core).
Axes of the slice: x: 2, y: 2, z: 4, core: 2. Of those that a mesh axis runs over, the one named last changes fastest.
Arguments:
- science: float32 [8, 32, 1024], P('epoch', 'vel'), may hold values from -6 to 6
- variance: float32 [8, 32, 1024], P('epoch', 'vel'), may hold values from 0.25 to 4
- psf: float32 [8, 9], P('epoch'), may hold values from 0.05 to 1
- shifts: int32 [2, 8, 8], P(None, None, 'vel'), may hold values from -16 to 16, as said below
Outputs:
- likelihood: float32 [8, 32, 1024], P('vel', 'epoch')
Inputs may be any that keep to these rules, and one draw needn't show every extreme that they name: For each velocity, the shifts of epoch e are the floor of the velocity's integer rates times the epoch's time over the span of the times; the first epoch's shifts are zero, and times rise with the epoch.
All inputs are finite; a program needn't handle non-finite values.
Results may differ from a plain program's by a relative error of at most 0.0003.
Values sent between devices are 32-bit elements; how exact they have to be, the bound alone decides.
No kernel may reach another device: no remote copies, remote signals or barrier semaphores. Data moves between devices by JAX's collectives and lax.ppermute only.
A program may use at most 64 MiB of HBM per device.

v0:
```python
import jax
import jax.numpy as jnp
from jax import lax
from jax.sharding import PartitionSpec as P

MAXS = 16


def extended(block, sides, width):
    for axis, dim in sides:
        count = lax.axis_size(axis)
        forward = [(i, i + 1) for i in range(count - 1)]
        backward = [(target, source) for source, target in forward]
        low = lax.ppermute(
            lax.slice_in_dim(block, block.shape[dim] - width, None, axis=dim), axis, forward
        )
        high = lax.ppermute(lax.slice_in_dim(block, 0, width, axis=dim), axis, backward)
        block = jnp.concatenate([low, block, high], axis=dim)
    return block


def filter_columns(pairing, weights):
    radius = weights.shape[2] // 2
    breadth = pairing.shape[3]
    padded = jnp.pad(pairing, ((0, 0), (0, 0), (0, 0), (radius, radius)))
    summed = jnp.zeros_like(pairing)
    for offset in range(weights.shape[2]):
        summed = (
            summed + weights[:, :, offset, None, None] * padded[:, :, :, offset : offset + breadth]
        )
    return summed


def filter_rows(rimmed, weights, height):
    summed = jnp.zeros(rimmed.shape[:2] + (height, rimmed.shape[3]), jnp.float32)
    for offset in range(weights.shape[2]):
        summed = (
            summed + weights[:, :, offset, None, None] * rimmed[:, :, offset : offset + height, :]
        )
    return summed


def per_device(science, variance, psf, shifts):
    slots = science.shape[0]
    height = science.shape[1]
    breadth = science.shape[2]
    radius = psf.shape[1] // 2
    pairing = jnp.stack([science / variance, 1.0 / variance], axis=1)
    weights = jnp.stack([psf, psf * psf], axis=1)
    columns_pass = filter_columns(pairing, weights)
    rimmed = extended(columns_pass, (("vel", 2),), radius)
    filtered = filter_rows(rimmed, weights, height)
    local_shifts = lax.dynamic_slice_in_dim(shifts, lax.axis_index("epoch") * slots, slots, 1)
    velocities = shifts.shape[2]
    gathered = lax.all_gather(filtered, "vel", axis=2, tiled=True)
    rows_all = gathered.shape[2]
    padded = jnp.pad(gathered, ((0, 0), (0, 0), (MAXS, MAXS), (MAXS, MAXS)))
    stacks = jnp.zeros((velocities, 2, rows_all, breadth), jnp.float32)
    for epoch_slot in range(slots):
        image = padded[epoch_slot]

        def window_at(shift_col, shift_row):
            return lax.dynamic_slice(
                image, (jnp.int32(0), MAXS + shift_row, MAXS + shift_col), (2, rows_all, breadth)
            )

        stacks = stacks + jax.vmap(window_at)(
            local_shifts[0, epoch_slot], local_shifts[1, epoch_slot]
        )
    mine = lax.psum_scatter(stacks, "epoch", scatter_dimension=2, tiled=True)
    return mine[:, 0] / jnp.sqrt(mine[:, 1])


def solution(mesh):
    return jax.shard_map(
        per_device,
        mesh=mesh,
        in_specs=(
            P("epoch", "vel", None),
            P("epoch", "vel", None),
            P("epoch", None),
            P(None, None, "vel"),
        ),
        out_specs=P("vel", "epoch", None),
        check_vma=False,
    )
```

profile of v0, /device:TPU:0, one launch (start us, length us, event | category | flops | bytes accessed | tf_op | source)
XLA Modules:
  0.0 81.5 jit_solution(1506419152563569825)
XLA Ops:
  6.5 0.0 all-reduce.5.cloned.1.call-start
  6.5 0.7 multiply_bitcast_fusion
  7.2 1.1 %fusion.26 = (f32[2,2,1]{2,0,1:T(2,128)S(1)}, f32[2,2,1]{2,0,1:T(2,128)S(1)}, f32[2,2,1]{2,0,1:T(2,128)S(1)}, f32[2,2,1]{2,0,1:T(2,128)S(1)}, f32[2,2,1]{2,0,1:T...) fusion(f32[2,1,9]{2,0,1:T(2,128)} %bitcast.58, ...), kind=kLoop, calls=%fused_computation.63 | loop fusion | flops 36 | bytes 288 | tf_op jit(solution)/shard_map/stack | solution.py:49
  8.3 0.1 copy.63
  8.4 0.1 copy.64
  8.5 0.1 copy.65
  8.6 0.1 copy.66
  8.7 0.1 copy.67
  8.8 0.1 copy.68
  8.9 0.1 copy.60
  9.0 0.1 copy.61
  9.1 0.1 copy.62
  9.2 0.8 divide_bitcast_fusion.1
  10.0 0.4 multiply_add_fusion
  10.4 2.4 %collective-permute-start = (f32[2,2,4,1024]{3,2,0,1:T(4,128)S(1)}, f32[2,2,4,1024]{3,2,0,1:T(4,128)S(1)}, u32[]{:S(2)}, u32[]{:S(2)}) collective-permute-start(f32[2,2,4,1024]{3,2,0,1:T(4,128)S(1)} %multiply_add_fusion), channel_id=1, source_target_pairs={{0,1},{1,2},{2,3},{3,4},{4,5},{5,6},{6,7},{8,9},{9,10},{10,11},{11... | collective-permute-start | bytes 196616 | tf_op jit(solution)/shard_map/ppermute | solution.py:14
  12.8 1.3 %collective-permute-start.1 = (f32[2,2,4,1024]{3,2,0,1:T(4,128)S(1)}, f32[2,2,4,1024]{3,2,0,1:T(4,128)S(1)}, u32[]{:S(2)}, u32[]{:S(2)}) collective-permute-start(f32[2,2,4,1024]{3,2,0,1:T(4,128)S(1)} %multiply_add_fusion), channel_id=1, source_target_pairs={{1,0},{2,1},{3,2},{4,3},{5,4},{6,5},{7,6},{9,8},{10,9},{11,10},{12... | collective-permute-start | bytes 196616 | tf_op jit(solution)/shard_map/ppermute | solution.py:17
  14.1 1.4 %constant_dynamic-slice_fusion = (s32[1,1,1]{1,2,0:T(1,128)}, s32[1,1,1]{1,2,0:T(1,128)}, s32[1,1,1]{1,2,0:T(1,128)}, s32[1,1,1]{1,2,0:T(1,128)}) fusion(s32[2,8,1]{1,2,0:T(1,128)} %param.7, s32[]{:T(128)S(6)} %select_n.15, s32[]{:T(128)S(6)} %add.166, s32[]{:T(128)S(6)} %add.168), kind=kLoop, calls=%fused_computation.71 | loop fusion | bytes 44 | tf_op jit(solution)/shard_map/slice | solution.py:68
  20.4 0.0 collective-permute-done
  20.5 0.0 collective-permute-done.1
  20.5 0.3 fusion.4
  20.7 0.1 copy.58
  20.8 14.1 %all_gather.3 = f32[2,2,32,1024]{3,1,0,2:T(2,128)S(1)} all-gather(f32[2,2,4,1024]{3,1,0,2:T(2,128)S(1)} %copy.58), channel_id=1, replica_groups=mesh['epoch'=4,'vel'=8] {'vel'}, dimensions={2}, use_global_device_ids=true | all-gather | bytes 589824 | tf_op jit(solution)/shard_map/all_gather | solution.py:55
  34.9 0.7 pad_slice_fusion.1
  35.6 0.0 copy-start
  35.7 1.3 %dynamic-slice_add_fusion = f32[1,2,32,1024]{3,1,0,2:T(2,128)} fusion(f32[1,2,64,1056]{3,1,0,2:T(2,128)S(1)} %get-tuple-element.28, s32[]{:T(128)} %bitcast.30, s32[]{:T(128)} %bitcast.33, f32[1,2,64,1056]{3,1,0,2:T(2,128)S(1)} %get-tuple-element.27, s32[]{:T(128)} %bitcast.24, s32[]{:T(128)} %bitcast.27), kind=kLoop, calls=%fused_computation.2 | loop fusion | flops 65536 | bytes 786448 | tf_op jit(solution)/shard_map/add | solution.py:67
  37.0 0.0 all-reduce.5.cloned.1.call-update
  37.0 0.0 copy-done
  37.0 0.6 dynamic-slice.10
  38.3 34.8 %all-reduce.5.cloned.1.call-done = f32[1,2,32,1024]{3,1,0,2:T(2,128)} async-done(((f32[1,2,32,1024]{3,1,0,2:T(2,128)}), f32[1,2,32,1024]{3,1,0,2:T(2,128)}) %all-reduce.5.cloned.1.call-update) | async-done | bytes 262160
  73.0 1.0 %fusion.24 = f32[1,8,1024]{2,0,1:T(1,128)S(1)} fusion(f32[1,2,32,1024]{3,1,0,2:T(2,128)} %all-reduce.5.cloned.1.call-done, u32[]{:T(128)S(6)} %convert, u32[]{:T(128)S(6)} %multiply.11), kind=kLoop, calls=%fused_computation.45 | loop fusion | flops 8192 | bytes 98312 | tf_op jit(solution)/shard_map/div | solution.py:71
  74.0 0.6 copy.59
  (1 shorter events, 0.0 us)
Async XLA Ops:
  6.5 66.5 %all-reduce.5.cloned.1.call-start = ((), (), s32[]{:S(2)}) async-start(), calls=%async_computation | async-start | bytes 524288
  10.4 10.0 %collective-permute-start = (f32[2,2,4,1024]{3,2,0,1:T(4,128)S(1)}, f32[2,2,4,1024]{3,2,0,1:T(4,128)S(1)}, u32[]{:S(2)}, u32[]{:S(2)}) collective-permute-start(f32[2,2,4,1024]{3,2,0,1:T(4,128)S(1)} %multiply_add_fusion), channel_id=1, source_target_pairs={{0,1},{1,2},{2,3},{3,4},{4,5},{5,6},{6,7},{8,9},{9,10},{10,11},{11... | collective-permute-start | bytes 196616 | tf_op jit(solution)/shard_map/ppermute | solution.py:14
  12.8 7.6 %collective-permute-start.1 = (f32[2,2,4,1024]{3,2,0,1:T(4,128)S(1)}, f32[2,2,4,1024]{3,2,0,1:T(4,128)S(1)}, u32[]{:S(2)}, u32[]{:S(2)}) collective-permute-start(f32[2,2,4,1024]{3,2,0,1:T(4,128)S(1)} %multiply_add_fusion), channel_id=1, source_target_pairs={{1,0},{2,1},{3,2},{4,3},{5,4},{6,5},{7,6},{9,8},{10,9},{11,10},{12... | collective-permute-start | bytes 196616 | tf_op jit(solution)/shard_map/ppermute | solution.py:17
  35.6 1.4 %copy-start = (u32[32]{0:T(128)S(1)}, u32[32]{0:T(128)}, u32[]{:S(2)}) copy-start(u32[32]{0:T(128)} %constant.89) | copy-start | bytes 388
Sparse Core Ops, SparseCore 0:
  37.1 35.8 all-reduce.4
where the time goes:
time: 81.9 us; the launch traced here: 81.5 us
  waiting for transfers between devices  34.8 us (42%)
  between operations  19.1 us (23%)
  blocking collectives  14.1 us (17%)
  other arithmetic  5.5 us (7%)
  local copies, waits for them, and re-layouts  4.27 us (5%)
  starting transfers between devices  3.69 us (5%)
    unnamed x2, waiting for transfers between devices  34.8 us
    all_gather x1, blocking collectives, per_device(): gathered = lax.all_gather(filtered, 'vel', axis=2, tiled=True)  14.1 us
    ppermute x1, starting transfers between devices, extended(): lax.ppermute(lax.slice_in_dim(block, block.shape[dim] - width, None, axis...  2.4 us
    another operation x2, other arithmetic, per_device(): weights = jnp.stack([psf, psf * psf], axis=1)  1.77 us
  transfers between devices with their start and end apart: 3, of which 1 were waited for; matrix products, arithmetic and copies ran while one was open for 2% of the time, Pallas kernels for 0%

commit v1 on v0

--- a/solution.py
+++ b/solution.py
@@ -52,7 +52,13 @@
     filtered = filter_rows(rimmed, weights, height)
     local_shifts = lax.dynamic_slice_in_dim(shifts, lax.axis_index("epoch") * slots, slots, 1)
     velocities = shifts.shape[2]
-    gathered = lax.all_gather(filtered, "vel", axis=2, tiled=True)
+    size = lax.axis_size("vel")
+    held, shards = (filtered, [filtered])
+    for _ in range(size - 1):
+        held = lax.ppermute(held, "vel", [(i_2, (i_2 + 1) % size) for i_2 in range(size)])
+        shards.insert(0, held)
+    row_of_blocks = jnp.concatenate(shards, axis=2)
+    gathered = jnp.roll(row_of_blocks, (lax.axis_index("vel") + 1) * filtered.shape[2], axis=2)
     rows_all = gathered.shape[2]
     padded = jnp.pad(gathered, ((0, 0), (0, 0), (MAXS, MAXS), (MAXS, MAXS)))
     stacks = jnp.zeros((velocities, 2, rows_all, breadth), jnp.float32)

time: 81.9 us -> 86.9 us (1.061)
  waiting for transfers between devices: 34.8 us -> 52.5 us
  blocking collectives: 14.1 us -> 0 us
  starting transfers between devices: 3.69 us -> 6.7 us
  local copies, waits for them, and re-layouts: 4.27 us -> 3.05 us
    unnamed x2 -> x1, waiting for transfers between devices: 34.8 us -> 0.02 us
    ppermute x0 -> x7, waiting for transfers between devices: none -> 24.6 us  [per_device(): lax.ppermute(held, 'vel', [(i_2, (i_2 + 1) % size) for i_2 in range(size)])]
    reduce_scatter x0 -> x1, waiting for transfers between devices: none -> 23.9 us  [per_device(): mine = lax.psum_scatter(stacks, 'epoch', scatter_dimension=2, tiled=True)]
    all_gather x1 -> x0, blocking collectives: 14.1 us -> none  [per_device(): gathered = lax.all_gather(filtered, 'vel', axis=2, tiled=True)]
    ppermute x1, waiting for transfers between devices: 0.01 us -> 3.93 us  [extended(): lax.ppermute(lax.slice_in_dim(block, 0, width, axis=dim), axis, backward)]
    ppermute x0 -> x7, starting transfers between devices: none -> 3 us  [per_device(): lax.ppermute(held, 'vel', [(i_2, (i_2 + 1) % size) for i_2 in range(size)])]
    slice x0 -> x9, local copies, waits for them, and re-layouts: none -> 0.88 us  [the longest x8 0.78 us: filter_columns(): weights[:, :, offset, None, None] * padded[:, :, :, offset:offset + breadth]]
    mul x9 -> x0, local copies, waits for them, and re-layouts: 0.88 us -> none  [the longest x8 0.78 us: filter_columns(): weights[:, :, offset, None, None] * padded[:, :, :, offset:offset + breadth]]
  transfers between devices with their start and end apart: 3 -> 10, of which waited for: 1 -> 8; matrix products, arithmetic and copies ran while one was open for 2% -> 2% of each run, Pallas kernels for 0% -> 0%
where the time goes in v1:
time: 86.9 us; the launch traced here: 86.5 us
  waiting for transfers between devices  52.5 us (60%)
  between operations  18.7 us (22%)
  starting transfers between devices  6.7 us (8%)
  other arithmetic  5.53 us (6%)
  local copies, waits for them, and re-layouts  3.05 us (4%)
    ppermute x7, waiting for transfers between devices, per_device(): lax.ppermute(held, 'vel', [(i_2, (i_2 + 1) % size) for i_2 in range(size)])  24.6 us
    reduce_scatter x1, waiting for transfers between devices, per_device(): mine = lax.psum_scatter(stacks, 'epoch', scatter_dimension=2, tiled=True)  23.9 us
    ppermute x1, waiting for transfers between devices, extended(): lax.ppermute(lax.slice_in_dim(block, 0, width, axis=dim), axis, backward)  3.93 us
    ppermute x7, starting transfers between devices, per_device(): lax.ppermute(held, 'vel', [(i_2, (i_2 + 1) % size) for i_2 in range(size)])  3 us
    ppermute x1, starting transfers between devices, extended(): lax.ppermute(lax.slice_in_dim(block, block.shape[dim] - width, None, axis...  2.4 us
    another operation x2, other arithmetic, per_device(): weights = jnp.stack([psf, psf * psf], axis=1)  1.77 us
  transfers between devices with their start and end apart: 10, of which 8 were waited for; matrix products, arithmetic and copies ran while one was open for 2% of the time, Pallas kernels for 0%

profile of v1, /device:TPU:0, one launch (start us, length us, event | category | flops | bytes accessed | tf_op | source)
XLA Modules:
  0.0 86.5 jit_solution(8333634695265740697)
XLA Ops:
  6.5 0.7 multiply_bitcast_fusion
  7.2 1.1 %fusion.26 = (f32[2,2,1]{2,0,1:T(2,128)S(1)}, f32[2,2,1]{2,0,1:T(2,128)S(1)}, f32[2,2,1]{2,0,1:T(2,128)S(1)}, f32[2,2,1]{2,0,1:T(2,128)S(1)}, f32[2,2,1]{2,0,1:T...) fusion(f32[2,1,9]{2,0,1:T(2,128)} %bitcast.48, ...), kind=kLoop, calls=%fused_computation.63 | loop fusion | flops 36 | bytes 288 | tf_op jit(solution)/shard_map/stack | solution.py:49
  8.3 0.1 copy.11
  8.4 0.1 copy.12
  8.5 0.1 copy.13
  8.6 0.1 copy.5
  8.7 0.1 copy.6
  8.8 0.1 copy.7
  8.9 0.1 copy.8
  9.0 0.1 copy.9
  9.1 0.1 copy.10
  9.2 0.8 divide_bitcast_fusion.1
  10.0 0.4 multiply_add_fusion
  10.4 2.4 %collective-permute-start = (f32[2,2,4,1024]{3,2,1,0:T(4,128)S(1)}, f32[2,2,4,1024]{3,2,1,0:T(4,128)S(1)}, u32[]{:S(2)}, u32[]{:S(2)}) collective-permute-start(f32[2,2,4,1024]{3,2,1,0:T(4,128)S(1)} %multiply_add_fusion), channel_id=1, source_target_pairs={{0,1},{1,2},{2,3},{3,4},{4,5},{5,6},{6,7},{8,9},{9,10},{10,11},{11... | collective-permute-start | bytes 196616 | tf_op jit(solution)/shard_map/ppermute | solution.py:14
  12.8 1.3 %collective-permute-start.1 = (f32[2,2,4,1024]{3,2,1,0:T(4,128)S(1)}, f32[2,2,4,1024]{3,2,1,0:T(4,128)S(1)}, u32[]{:S(2)}, u32[]{:S(2)}) collective-permute-start(f32[2,2,4,1024]{3,2,1,0:T(4,128)S(1)} %multiply_add_fusion), channel_id=1, source_target_pairs={{1,0},{2,1},{3,2},{4,3},{5,4},{6,5},{7,6},{9,8},{10,9},{11,10},{12... | collective-permute-start | bytes 196616 | tf_op jit(solution)/shard_map/ppermute | solution.py:17
  14.1 3.9 %collective-permute-done.1 = f32[2,2,4,1024]{3,2,1,0:T(4,128)S(1)} collective-permute-done((f32[2,2,4,1024]{3,2,1,0:T(4,128)S(1)}, f32[2,2,4,1024]{3,2,1,0:T(4,128)S(1)}, u32[]{:S(2)}, u32[]{:S(2)}) %collective-permute-start.1) | collective-permute-done | bytes 65568 | tf_op jit(solution)/shard_map/ppermute | solution.py:17
  18.1 0.3 fusion.4
  18.3 3.0 %collective-permute-start.2 = (f32[2,2,4,1024]{3,2,1,0:T(4,128)S(1)}, f32[2,2,4,1024]{3,2,1,0:T(4,128)S(1)}, u32[]{:S(2)}, u32[]{:S(2)}) collective-permute-start(f32[2,2,4,1024]{3,2,1,0:T(4,128)S(1)} %fusion.4), channel_id=1, source_target_pairs={{0,1},{1,2},{2,3},{3,4},{4,5},{5,6},{6,7},{7,0},{8,9},{9,10},{10,1... | collective-permute-start | bytes 196616 | tf_op jit(solution)/shard_map/ppermute | solution.py:58
  21.3 1.7 %collective-permute-done.2 = f32[2,2,4,1024]{3,2,1,0:T(4,128)S(1)} collective-permute-done((f32[2,2,4,1024]{3,2,1,0:T(4,128)S(1)}, f32[2,2,4,1024]{3,2,1,0:T(4,128)S(1)}, u32[]{:S(2)}, u32[]{:S(2)}) %collective-permute-start.2) | collective-permute-done | bytes 65568 | tf_op jit(solution)/shard_map/ppermute | solution.py:58
  23.0 4.6 %collective-permute-done.3 = f32[2,2,4,1024]{3,2,1,0:T(4,128)S(1)} collective-permute-done((f32[2,2,4,1024]{3,2,1,0:T(4,128)S(1)}, f32[2,2,4,1024]{3,2,1,0:T(4,128)S(1)}, u32[]{:S(2)}, u32[]{:S(2)}) %collective-permute-start.3) | collective-permute-done | bytes 65568 | tf_op jit(solution)/shard_map/ppermute | solution.py:58
  27.5 4.6 %collective-permute-done.4 = f32[2,2,4,1024]{3,2,1,0:T(4,128)S(1)} collective-permute-done((f32[2,2,4,1024]{3,2,1,0:T(4,128)S(1)}, f32[2,2,4,1024]{3,2,1,0:T(4,128)S(1)}, u32[]{:S(2)}, u32[]{:S(2)}) %collective-permute-start.4) | collective-permute-done | bytes 65568 | tf_op jit(solution)/shard_map/ppermute | solution.py:58
  32.1 4.6 %collective-permute-done.5 = f32[2,2,4,1024]{3,2,1,0:T(4,128)S(1)} collective-permute-done((f32[2,2,4,1024]{3,2,1,0:T(4,128)S(1)}, f32[2,2,4,1024]{3,2,1,0:T(4,128)S(1)}, u32[]{:S(2)}, u32[]{:S(2)}) %collective-permute-start.5) | collective-permute-done | bytes 65568 | tf_op jit(solution)/shard_map/ppermute | solution.py:58
  36.7 4.6 %collective-permute-done.6 = f32[2,2,4,1024]{3,2,1,0:T(4,128)S(1)} collective-permute-done((f32[2,2,4,1024]{3,2,1,0:T(4,128)S(1)}, f32[2,2,4,1024]{3,2,1,0:T(4,128)S(1)}, u32[]{:S(2)}, u32[]{:S(2)}) %collective-permute-start.6) | collective-permute-done | bytes 65568 | tf_op jit(solution)/shard_map/ppermute | solution.py:58
  41.3 4.6 %collective-permute-done.7 = f32[2,2,4,1024]{3,2,1,0:T(4,128)S(1)} collective-permute-done((f32[2,2,4,1024]{3,2,1,0:T(4,128)S(1)}, f32[2,2,4,1024]{3,2,1,0:T(4,128)S(1)}, u32[]{:S(2)}, u32[]{:S(2)}) %collective-permute-start.7) | collective-permute-done | bytes 65568 | tf_op jit(solution)/shard_map/ppermute | solution.py:58
  45.9 1.4 %constant_dynamic-slice_fusion = (s32[1,1,1]{1,2,0:T(1,128)}, s32[1,1,1]{1,2,0:T(1,128)}, s32[1,1,1]{1,2,0:T(1,128)}, s32[1,1,1]{1,2,0:T(1,128)}) fusion(s32[2,8,1]{1,2,0:T(1,128)} %param.7, s32[]{:T(128)S(6)} %select_n.30, s32[]{:T(128)S(6)} %add.180, s32[]{:T(128)S(6)} %add.182), kind=kLoop, calls=%fused_computation.71 | loop fusion | bytes 44 | tf_op jit(solution)/shard_map/slice | solution.py:74
  52.5 0.5 concatenate.25
  53.0 0.1 constant_dynamic-slice_fusion.4
  53.1 0.2 pad_slice_fusion.1
  53.3 0.9 %dynamic-slice_add_fusion = f32[1,2,32,1024]{3,2,1,0:T(8,128)} fusion(f32[1,2,64,1056]{3,2,1,0:T(8,128)S(1)} %get-tuple-element.28, s32[]{:T(128)} %bitcast.21, s32[]{:T(128)} %bitcast.24, f32[1,2,64,1056]{3,2,1,0:T(8,128)S(1)} %get-tuple-element.27, s32[]{:T(128)} %bitcast.15, s32[]{:T(128)} %bitcast.18), kind=kLoop, calls=%fused_computation.2 | loop fusion | flops 65536 | bytes 786448 | tf_op jit(solution)/shard_map/add | solution.py:73
  54.2 0.0 reduce-scatter.2.cloned.1.call-update
  54.3 23.9 %reduce-scatter.2.cloned.1.call-done = f32[1,2,8,1024]{3,2,1,0:T(8,128)} async-done(((f32[1,2,32,1024]{3,2,1,0:T(8,128)}), f32[1,2,8,1024]{3,2,1,0:T(8,128)}) %reduce-scatter.2.cloned.1.call-update) | async-done | bytes 65552 | tf_op jit(solution)/shard_map/reduce_scatter | solution.py:76
  78.2 1.4 %fusion.24 = f32[1,8,1024]{2,1,0:T(8,128)} fusion(f32[1,2,8,1024]{3,2,1,0:T(8,128)} %reduce-scatter.2.cloned.1.call-done), kind=kLoop, calls=%fused_computation.43 | loop fusion | flops 8192 | bytes 98304 | tf_op jit(solution)/shard_map/div | solution.py:77
  (10 shorter events, 0.0 us)
Async XLA Ops:
  6.5 71.7 %reduce-scatter.2.cloned.1.call-start = ((), (), s32[]{:S(2)}) async-start(), calls=%async_computation.1 | async-start | bytes 327680 | tf_op jit(solution)/shard_map/reduce_scatter | solution.py:76
  10.4 3.7 %collective-permute-start = (f32[2,2,4,1024]{3,2,1,0:T(4,128)S(1)}, f32[2,2,4,1024]{3,2,1,0:T(4,128)S(1)}, u32[]{:S(2)}, u32[]{:S(2)}) collective-permute-start(f32[2,2,4,1024]{3,2,1,0:T(4,128)S(1)} %multiply_add_fusion), channel_id=1, source_target_pairs={{0,1},{1,2},{2,3},{3,4},{4,5},{5,6},{6,7},{8,9},{9,10},{10,11},{11... | collective-permute-start | bytes 196616 | tf_op jit(solution)/shard_map/ppermute | solution.py:14
  12.8 5.2 %collective-permute-start.1 = (f32[2,2,4,1024]{3,2,1,0:T(4,128)S(1)}, f32[2,2,4,1024]{3,2,1,0:T(4,128)S(1)}, u32[]{:S(2)}, u32[]{:S(2)}) collective-permute-start(f32[2,2,4,1024]{3,2,1,0:T(4,128)S(1)} %multiply_add_fusion), channel_id=1, source_target_pairs={{1,0},{2,1},{3,2},{4,3},{5,4},{6,5},{7,6},{9,8},{10,9},{11,10},{12... | collective-permute-start | bytes 196616 | tf_op jit(solution)/shard_map/ppermute | solution.py:17
  18.3 4.6 %collective-permute-start.2 = (f32[2,2,4,1024]{3,2,1,0:T(4,128)S(1)}, f32[2,2,4,1024]{3,2,1,0:T(4,128)S(1)}, u32[]{:S(2)}, u32[]{:S(2)}) collective-permute-start(f32[2,2,4,1024]{3,2,1,0:T(4,128)S(1)} %fusion.4), channel_id=1, source_target_pairs={{0,1},{1,2},{2,3},{3,4},{4,5},{5,6},{6,7},{7,0},{8,9},{9,10},{10,1... | collective-permute-start | bytes 196616 | tf_op jit(solution)/shard_map/ppermute | solution.py:58
  23.0 4.6 %collective-permute-start.3 = (f32[2,2,4,1024]{3,2,1,0:T(4,128)S(1)}, f32[2,2,4,1024]{3,2,1,0:T(4,128)S(1)}, u32[]{:S(2)}, u32[]{:S(2)}) collective-permute-start(f32[2,2,4,1024]{3,2,1,0:T(4,128)S(1)} %collective-permute-done.2), channel_id=1, source_target_pairs={{0,1},{1,2},{2,3},{3,4},{4,5},{5,6},{6,7},{7,0},{8,9},{9,10},{10,1... | collective-permute-start | bytes 196616 | tf_op jit(solution)/shard_map/ppermute | solution.py:58
  27.5 4.6 %collective-permute-start.4 = (f32[2,2,4,1024]{3,2,1,0:T(4,128)S(1)}, f32[2,2,4,1024]{3,2,1,0:T(4,128)S(1)}, u32[]{:S(2)}, u32[]{:S(2)}) collective-permute-start(f32[2,2,4,1024]{3,2,1,0:T(4,128)S(1)} %collective-permute-done.3), channel_id=1, source_target_pairs={{0,1},{1,2},{2,3},{3,4},{4,5},{5,6},{6,7},{7,0},{8,9},{9,10},{10,1... | collective-permute-start | bytes 196616 | tf_op jit(solution)/shard_map/ppermute | solution.py:58
  32.1 4.6 %collective-permute-start.5 = (f32[2,2,4,1024]{3,2,1,0:T(4,128)S(1)}, f32[2,2,4,1024]{3,2,1,0:T(4,128)S(1)}, u32[]{:S(2)}, u32[]{:S(2)}) collective-permute-start(f32[2,2,4,1024]{3,2,1,0:T(4,128)S(1)} %collective-permute-done.4), channel_id=1, source_target_pairs={{0,1},{1,2},{2,3},{3,4},{4,5},{5,6},{6,7},{7,0},{8,9},{9,10},{10,1... | collective-permute-start | bytes 196616 | tf_op jit(solution)/shard_map/ppermute | solution.py:58
  36.7 4.6 %collective-permute-start.6 = (f32[2,2,4,1024]{3,2,1,0:T(4,128)S(1)}, f32[2,2,4,1024]{3,2,1,0:T(4,128)S(1)}, u32[]{:S(2)}, u32[]{:S(2)}) collective-permute-start(f32[2,2,4,1024]{3,2,1,0:T(4,128)S(1)} %collective-permute-done.5), channel_id=1, source_target_pairs={{0,1},{1,2},{2,3},{3,4},{4,5},{5,6},{6,7},{7,0},{8,9},{9,10},{10,1... | collective-permute-start | bytes 196616 | tf_op jit(solution)/shard_map/ppermute | solution.py:58
  41.3 4.6 %collective-permute-start.7 = (f32[2,2,4,1024]{3,2,1,0:T(4,128)S(1)}, f32[2,2,4,1024]{3,2,1,0:T(4,128)S(1)}, u32[]{:S(2)}, u32[]{:S(2)}) collective-permute-start(f32[2,2,4,1024]{3,2,1,0:T(4,128)S(1)} %collective-permute-done.6), channel_id=1, source_target_pairs={{0,1},{1,2},{2,3},{3,4},{4,5},{5,6},{6,7},{7,0},{8,9},{9,10},{10,1... | collective-permute-start | bytes 196616 | tf_op jit(solution)/shard_map/ppermute | solution.py:58
  45.9 6.6 %collective-permute-start.8 = (f32[2,2,4,1024]{3,2,1,0:T(4,128)S(1)}, f32[2,2,4,1024]{3,2,1,0:T(4,128)S(1)}, u32[]{:S(2)}, u32[]{:S(2)}) collective-permute-start(f32[2,2,4,1024]{3,2,1,0:T(4,128)S(1)} %collective-permute-done.7), channel_id=1, source_target_pairs={{0,1},{1,2},{2,3},{3,4},{4,5},{5,6},{6,7},{7,0},{8,9},{9,10},{10,1... | collective-permute-start | bytes 196616 | tf_op jit(solution)/shard_map/ppermute | solution.py:58
Sparse Core Ops, SparseCore 0:
  54.4 23.7 reduce-scatter.1
